TPU v7x, 32 devices: a whole 2x2x4 slice. The times are simulated.
32 devices in a mesh: row: 2 (over x), col: 16 (over z, y, core).
Axes of the slice: x: 2, y: 2, z: 4, core: 2. Of those that a mesh axis runs over, the one named last changes fastest.
Arguments:
- coords: float32 [64, 3, 256], P(('row', 'col')), may hold values from 0 to 8, as said below
- noise_var: float32 [64, 256], P(('row', 'col')), may hold values from 0.1 to 1
- right_side: float32 [64, 8, 256], P(('row', 'col')), may hold values from -32 to 32
- start_guess: float32 [64, 8, 256], P(('row', 'col')), may hold values from -3 to 3
- tile_pairs: int32 [2, 16, 2, 63], P('row', 'col'), may hold values from -1 to 31, as said below
Outputs:
- solution_field: float32 [64, 8, 256], P(('row', 'col'))
- residual: float32 [64, 8, 256], P(('row', 'col'))
Inputs may be any that keep to these rules, and one draw needn't show every extreme that they name: `coords`: each tile's points lie within one unit cell of the integer lattice, and distinct tiles lie in distinct cells. `tile_pairs`: each device's list holds every pair of its block whose cells differ by at most one in each coordinate, each pair once and no other; listed entries come first, then entries of -1 in both rows.
All inputs are finite; a program needn't handle non-finite values.
Results may differ from a plain program's by a relative error of at most 0.0003.
Values sent between devices are 32-bit elements; how exact they have to be, the bound alone decides.
A program may use at most 64 MiB of HBM per device.

v0:
```python
import jax
import jax.numpy as jnp
from jax import lax
from jax.sharding import PartitionSpec as P

ITERS = 3
pair_group = 2


def wendland(left_points, right_points):
    squared = jnp.zeros(
        (left_points.shape[0], left_points.shape[2], right_points.shape[2]), jnp.float32
    )
    for component in range(3):
        spacing = left_points[:, component, :, None] - right_points[:, component, None, :]
        squared = squared + spacing * spacing
    distance = jnp.sqrt(squared)
    remain = jnp.maximum(1.0 - distance, 0.0)
    return remain**4 * (4.0 * distance + 1.0)


def squares(residual):
    return lax.psum(jnp.sum(residual * residual, axis=(0, 2)), ("row", "col"))


def shards(coords, noise_var, right_side, start_guess, tile_pairs):
    row_points = lax.all_gather(coords, "col", axis=0, tiled=True)
    col_points = lax.all_gather(coords, "row", axis=0, tiled=True)
    row_count = row_points.shape[0]
    listed = tile_pairs[0, 0]
    usable = listed[0] >= 0
    sort_key = jnp.where(usable, listed[0], row_count)
    sorted_index = jnp.argsort(sort_key, stable=True)
    sorted_rows = jnp.concatenate(
        [sort_key[sorted_index], jnp.full((pair_group,), row_count, jnp.int32)]
    )
    sorted_cols = jnp.concatenate(
        [jnp.where(usable, listed[1], 0)[sorted_index], jnp.zeros((pair_group,), jnp.int32)]
    )

    def pair_range(first_row, row_number):
        first = jnp.sum(sorted_rows < first_row)
        last = jnp.sum(sorted_rows < first_row + row_number)
        return (first, last, (last - first + pair_group - 1) // pair_group)

    def group_weights(position, last):
        indices = position + jnp.arange(pair_group, dtype=jnp.int32)
        rows_group = lax.dynamic_slice_in_dim(sorted_rows, position, pair_group)
        cols_group = lax.dynamic_slice_in_dim(sorted_cols, position, pair_group)
        inside = (indices < last).astype(jnp.float32)
        safe_rows = jnp.minimum(rows_group, row_count - 1)
        weights = wendland(row_points[safe_rows], col_points[cols_group]) * inside[:, None, None]
        return (weights, safe_rows, cols_group)

    def apply_operator(vectors):
        empty = jnp.zeros((col_points.shape[0],) + vectors.shape[1:], jnp.float32)
        pieces = lax.all_gather(vectors, "col", axis=0, tiled=True)
        number = pieces.shape[0]
        first, last, turns = pair_range(jnp.int32(0), number)

        def visit(turn, running):
            weights, safe_rows, cols_group = group_weights(first + pair_group * turn, last)
            local_rows = jnp.clip(safe_rows, 0, number - 1)
            product = jnp.einsum(
                "pab,psa->psb", weights, pieces[local_rows], precision=lax.Precision.HIGHEST
            )
            return running.at[cols_group].add(product)

        gathered_sum = lax.fori_loop(0, turns, visit, empty)
        coupled = lax.psum_scatter(gathered_sum, "row", scatter_dimension=0, tiled=True)
        return coupled + noise_var[:, None, :] * vectors

    solution_field = start_guess
    residual = right_side - apply_operator(start_guess)
    direction = residual
    norm_now = squares(residual)
    for iteration in range(ITERS):
        applied = apply_operator(direction)
        step_size = norm_now / lax.psum(jnp.sum(direction * applied, axis=(0, 2)), ("row", "col"))
        solution_field = solution_field + step_size[None, :, None] * direction
        residual = residual - step_size[None, :, None] * applied
        norm_next = squares(residual)
        direction = residual + (norm_next / norm_now)[None, :, None] * direction
        norm_now = norm_next
    return (solution_field, residual)


def solution(mesh):
    placed = (
        P(("row", "col"), None, None),
        P(("row", "col"), None),
        P(("row", "col"), None, None),
        P(("row", "col"), None, None),
        P("row", "col", None, None),
    )
    return jax.shard_map(
        shards,
        mesh=mesh,
        in_specs=placed,
        out_specs=(P(("row", "col"), None, None), P(("row", "col"), None, None)),
        check_vma=False,
    )
```

profile of v0, /device:TPU:0, one launch (start us, length us, event | category | flops | bytes accessed | tf_op | source)
XLA Modules:
  0.0 646.0 jit_solution(4284149621219089081)
XLA Ops:
  8.0 2.0 sort.17
  13.5 23.5 %all_gather.19 = f32[32,3,256]{2,1,0:T(4,128)S(1)} all-gather(f32[2,3,256]{2,1,0:T(4,128)S(1)} %copy.11), channel_id=1, replica_groups=mesh['row'=2,'col'=16] {'col'}, dimensions={0}, use_global_device_ids=true | all-gather | bytes 104448 | tf_op jit(solution)/shard_map/all_gather | solution.py:27
  36.9 4.3 all_gather.20
  42.1 17.8 %all_gather.18 = f32[32,8,256]{2,1,0:T(8,128)S(1)} all-gather(f32[2,8,256]{2,1,0:T(8,128)S(1)} %copy-done.5), channel_id=1, replica_groups=mesh['row'=2,'col'=16] {'col'}, dimensions={0}, use_global_device_ids=true | all-gather | bytes 278528 | tf_op jit(solution)/shard_map/all_gather | solution.py:57
  59.9 55.7 %while.40 = (s32[]{:T(128)}, f32[4,8,256]{2,1,0:T(8,128)S(1)}, s32[]{:T(128)}, s32[]{:T(128)}, s32[65]{0:T(128)S(1)}, /*index=5*/s32[65]{0:T(128)S(1)}, f32[32,8...) while((s32[]{:T(128)}, f32[4,8,256]{2,1,0:T(8,128)S(1)}, ...), condition=%wide.region_5.6_spmd, body=%wide.region_3.5_spmd.sunk | while | flops 14687269 | bytes 213307 | solution.py:69
  116.3 22.8 %reduce-scatter.5.cloned.1.call-done = f32[2,8,256]{2,1,0:T(8,128)} async-done(((f32[4,8,256]{2,1,0:T(8,128)}), f32[2,8,256]{2,1,0:T(8,128)}) %reduce-scatter.5.cloned.1.call-update) | async-done | bytes 16400 | tf_op jit(solution)/shard_map/reduce_scatter | solution.py:70
  139.9 22.0 %all_gather.21 = f32[32,8,256]{2,1,0:T(8,128)S(1)} all-gather(f32[2,8,256]{2,1,0:T(8,128)S(1)} %add_subtract_fusion), channel_id=1, replica_groups=mesh['row'=2,'col'=16] {'col'}, dimensions={0}, use_global_device_ids=true | all-gather | bytes 278528 | tf_op jit(solution)/shard_map/all_gather | solution.py:57
  161.9 55.7 %while.41 = (s32[]{:T(128)}, f32[4,8,256]{2,1,0:T(8,128)S(1)}, s32[]{:T(128)}, s32[]{:T(128)}, s32[65]{0:T(128)S(1)}, /*index=5*/s32[65]{0:T(128)S(1)}, f32[32,8...) while((s32[]{:T(128)}, f32[4,8,256]{2,1,0:T(8,128)S(1)}, ...), condition=%wide.region_11.12_spmd, body=%wide.region_9.11_spmd.sunk | while | flops 14687269 | bytes 213307 | solution.py:69
  179.0 0.8 fusion.167
  218.3 20.3 %reduce-scatter.7.cloned.1.call-done = f32[2,8,256]{2,1,0:T(8,128)} async-done(((f32[4,8,256]{2,1,0:T(8,128)}), f32[2,8,256]{2,1,0:T(8,128)}) %reduce-scatter.7.cloned.1.call-update) | async-done | bytes 16400 | tf_op jit(solution)/shard_map/reduce_scatter | solution.py:70
  238.6 0.9 multiply_reduce_fusion.4
  239.5 39.3 %all-reduce.2 = (f32[8]{0:T(128)S(1)}, f32[8]{0:T(128)S(1)}) all-reduce(f32[8]{0:T(128)S(1)} %get-tuple-element.221, f32[8]{0:T(128)S(1)} %get-tuple-element.220), channel_id=1, replica_groups=mesh['row'=2,'col'=16] {'row','col'}, use_global_device_ids=true, to_apply=%region_8.9 | all-reduce | flops 16 | bytes 128 | tf_op jit(solution)/shard_map/psum | solution.py:23
  279.1 40.9 %psum.44 = f32[8]{0:T(128)S(1)} all-reduce(f32[8]{0:T(128)S(1)} %multiply_reduce_fusion.3), channel_id=1, replica_groups=mesh['row'=2,'col'=16] {'row','col'}, use_global_device_ids=true, to_apply=%region_16.17 | all-reduce | flops 8 | bytes 64 | tf_op jit(solution)/shard_map/psum | solution.py:23
  320.1 21.8 %all_gather.22 = f32[32,8,256]{2,1,0:T(8,128)S(1)} all-gather(f32[2,8,256]{2,1,0:T(8,128)S(1)} %multiply_add_fusion.4), channel_id=1, replica_groups=mesh['row'=2,'col'=16] {'col'}, dimensions={0}, use_global_device_ids=true | all-gather | bytes 278528 | tf_op jit(solution)/shard_map/all_gather | solution.py:57
  341.9 55.7 %while.42 = (s32[]{:T(128)}, f32[4,8,256]{2,1,0:T(8,128)S(1)}, s32[]{:T(128)}, s32[]{:T(128)}, s32[65]{0:T(128)S(1)}, /*index=5*/s32[65]{0:T(128)S(1)}, f32[32,8...) while((s32[]{:T(128)}, f32[4,8,256]{2,1,0:T(8,128)S(1)}, ...), condition=%wide.region_19.20_spmd, body=%wide.region_17.19_spmd.sunk | while | flops 14687269 | bytes 213307 | solution.py:69
  398.3 20.3 %reduce-scatter.9.cloned.1.call-done = f32[2,8,256]{2,1,0:T(8,128)} async-done(((f32[4,8,256]{2,1,0:T(8,128)}), f32[2,8,256]{2,1,0:T(8,128)}) %reduce-scatter.9.cloned.1.call-update) | async-done | bytes 16400 | tf_op jit(solution)/shard_map/reduce_scatter | solution.py:70
  418.6 0.9 multiply_reduce_fusion.2
  419.5 39.3 %psum.45 = f32[8]{0:T(128)S(1)} all-reduce(f32[8]{0:T(128)S(1)} %multiply_reduce_fusion.2), channel_id=1, replica_groups=mesh['row'=2,'col'=16] {'row','col'}, use_global_device_ids=true, to_apply=%region_22.23 | all-reduce | flops 8 | bytes 64 | tf_op jit(solution)/shard_map/psum | solution.py:79
  459.0 41.0 %psum.46 = f32[8]{0:T(128)S(1)} all-reduce(f32[8]{0:T(128)S(1)} %get-tuple-element.306), channel_id=1, replica_groups=mesh['row'=2,'col'=16] {'row','col'}, use_global_device_ids=true, to_apply=%region_24.25 | all-reduce | flops 8 | bytes 64 | tf_op jit(solution)/shard_map/psum | solution.py:23
  500.1 21.8 %all_gather.23 = f32[32,8,256]{2,1,0:T(8,128)S(1)} all-gather(f32[2,8,256]{2,1,0:T(8,128)S(1)} %multiply_add_fusion.2), channel_id=1, replica_groups=mesh['row'=2,'col'=16] {'col'}, dimensions={0}, use_global_device_ids=true | all-gather | bytes 278528 | tf_op jit(solution)/shard_map/all_gather | solution.py:57
  521.9 55.7 %while.43 = (s32[]{:T(128)}, f32[4,8,256]{2,1,0:T(8,128)S(1)}, s32[]{:T(128)}, s32[]{:T(128)}, s32[65]{0:T(128)S(1)}, /*index=5*/s32[65]{0:T(128)S(1)}, f32[32,8...) while((s32[]{:T(128)}, f32[4,8,256]{2,1,0:T(8,128)S(1)}, ...), condition=%wide.region_27.28_spmd, body=%wide.region_25.27_spmd.sunk | while | flops 14687269 | bytes 213307 | solution.py:69
  578.3 20.3 %reduce-scatter.11.cloned.1.call-done = f32[2,8,256]{2,1,0:T(8,128)} async-done(((f32[4,8,256]{2,1,0:T(8,128)}), f32[2,8,256]{2,1,0:T(8,128)}) %reduce-scatter.11.cloned.1.call-update) | async-done | bytes 16400 | tf_op jit(solution)/shard_map/reduce_scatter | solution.py:70
  598.6 0.9 multiply_reduce_fusion
  599.5 39.3 %psum.47 = f32[8]{0:T(128)S(1)} all-reduce(f32[8]{0:T(128)S(1)} %multiply_reduce_fusion), channel_id=1, replica_groups=mesh['row'=2,'col'=16] {'row','col'}, use_global_device_ids=true, to_apply=%region_30.31 | all-reduce | flops 8 | bytes 64 | tf_op jit(solution)/shard_map/psum | solution.py:79
  (917 shorter events, 194.2 us)
Async XLA Ops:
  7.2 132.0 %reduce-scatter.5.cloned.1.call-start = ((), (), s32[]{:S(2)}) async-start(), calls=%async_computation.4 | async-start | bytes 49152 | tf_op jit(solution)/shard_map/reduce_scatter | solution.py:70
  12.8 0.7 copy-start.10
  41.3 0.8 copy-start.5
  115.7 0.6 copy-start.1
  115.7 23.5 %copy-start.6 = (f32[2,256]{1,0:T(2,128)S(1)}, f32[2,256]{1,0:T(2,128)}, u32[]{:S(2)}) copy-start(f32[2,256]{1,0:T(2,128)} %param.14) | copy-start | bytes 6148
  115.7 23.5 %copy-start.9 = (f32[2,8,256]{2,1,0:T(8,128)S(1)}, f32[2,8,256]{2,1,0:T(8,128)}, u32[]{:S(2)}) copy-start(f32[2,8,256]{2,1,0:T(8,128)} %param.15) | copy-start | bytes 49156
  116.3 122.3 %reduce-scatter.7.cloned.1.call-start = ((), (), s32[]{:S(2)}) async-start(), calls=%async_computation.5 | async-start | bytes 49152 | tf_op jit(solution)/shard_map/reduce_scatter | solution.py:70
  217.6 0.6 copy-start.2
  218.2 200.4 %reduce-scatter.9.cloned.1.call-start = ((), (), s32[]{:S(2)}) async-start(), calls=%async_computation.6 | async-start | bytes 49152 | tf_op jit(solution)/shard_map/reduce_scatter | solution.py:70
  238.6 40.3 %copy-start.4 = (f32[2,8,256]{2,1,0:T(8,128)S(1)}, f32[2,8,256]{2,1,0:T(8,128)}, u32[]{:S(2)}) copy-start(f32[2,8,256]{2,1,0:T(8,128)} %reduce-scatter.7.cloned.1.call-done) | copy-start | bytes 49156
  397.6 0.6 copy-start.3
  398.3 200.3 %reduce-scatter.11.cloned.1.call-start = ((), (), s32[]{:S(2)}) async-start(), calls=%async_computation.7 | async-start | bytes 49152 | tf_op jit(solution)/shard_map/reduce_scatter | solution.py:70
  418.6 40.2 %copy-start.8 = (f32[2,8,256]{2,1,0:T(8,128)S(1)}, f32[2,8,256]{2,1,0:T(8,128)}, u32[]{:S(2)}) copy-start(f32[2,8,256]{2,1,0:T(8,128)} %reduce-scatter.9.cloned.1.call-done) | copy-start | bytes 49156
  577.6 0.6 copy-start
  598.6 40.2 %copy-start.7 = (f32[2,8,256]{2,1,0:T(8,128)S(1)}, f32[2,8,256]{2,1,0:T(8,128)}, u32[]{:S(2)}) copy-start(f32[2,8,256]{2,1,0:T(8,128)} %reduce-scatter.11.cloned.1.call-done) | copy-start | bytes 49156
Sparse Core Ops, SparseCore 0:
  116.4 22.6 reduce-scatter.4
  218.4 20.1 reduce-scatter.6
  398.4 20.1 reduce-scatter.8
  578.4 20.1 reduce-scatter.10
where the time goes:
time: 649 us; the launch traced here: 646 us
  blocking collectives  311 us (48%)
  local copies, waits for them, and re-layouts  87.6 us (13%)
  waiting for transfers between devices  83.8 us (13%)
  other arithmetic  72.8 us (11%)
  matrix products  39.1 us (6%)
  loops' own time  36.2 us (6%)
  between operations  15.2 us (2%)
    psum x3, blocking collectives, squares(): return lax.psum(jnp.sum(residual * residual, axis=(0, 2)), ('row', 'col'))  121 us
    reduce_scatter x4, waiting for transfers between devices, apply_operator(): lax.psum_scatter(gathered_sum, 'row', scatter_dimension=0, tiled=True)  83.7 us
    all_gather x4, blocking collectives, apply_operator(): pieces = lax.all_gather(vectors, 'col', axis=0, tiled=True)  83.5 us
    psum x2, blocking collectives, shards(): lax.psum(jnp.sum(direction * applied, axis=(0, 2)), ('row', 'col'))  78.6 us
    dot_general x48, matrix products, visit(): jnp.einsum('pab,psa->psb', weights, pieces[local_rows], precision=lax.Pre...  39.1 us
    another operation x4, loops' own time, apply_operator(): gathered_sum = lax.fori_loop(0, turns, visit, empty)  36.2 us
    convert_element_type x48, other arithmetic, group_weights(): inside = (indices < last).astype(jnp.float32)  30.5 us
    scatter-add x48, other arithmetic, visit(): return running.at[cols_group].add(product)  29.3 us
  transfers between devices with their start and end apart: 4, of which 4 were waited for; matrix products, arithmetic and copies ran while one was open for 0% of the time, Pallas kernels for 0%

commit v1 on v0

--- a/solution.py
+++ b/solution.py
@@ -5,6 +5,16 @@
 
 ITERS = 3
 pair_group = 2
+
+
+def gather_by_hops(value, axis, dim):
+    size = lax.axis_size(axis)
+    current, blocks = (value, [value])
+    for _ in range(size - 1):
+        current = lax.ppermute(current, axis, [(i, (i + 1) % size) for i in range(size)])
+        blocks.insert(0, current)
+    flat = jnp.concatenate(blocks, axis=dim)
+    return jnp.roll(flat, (lax.axis_index(axis) + 1) * value.shape[dim], axis=dim)
 
 
 def wendland(left_points, right_points):
@@ -54,7 +64,7 @@
 
     def apply_operator(vectors):
         empty = jnp.zeros((col_points.shape[0],) + vectors.shape[1:], jnp.float32)
-        pieces = lax.all_gather(vectors, "col", axis=0, tiled=True)
+        pieces = gather_by_hops(vectors, "col", 0)
         number = pieces.shape[0]
         first, last, turns = pair_range(jnp.int32(0), number)
 

time: 649 us -> 909 us (1.40)
  waiting for transfers between devices: 83.8 us -> 429 us
  blocking collectives: 311 us -> 223 us
    ppermute x0 -> x60, waiting for transfers between devices: none -> 342 us  [gather_by_hops(): lax.ppermute(current, axis, [(i, (i + 1) % size) for i in range(size)])]
    all_gather x4 -> x0, blocking collectives: 83.5 us -> none  [apply_operator(): pieces = lax.all_gather(vectors, 'col', axis=0, tiled=True)]
  transfers between devices with their start and end apart: 4 -> 64, of which waited for: 4 -> 63; matrix products, arithmetic and copies ran while one was open for 0% -> 1% of each run, Pallas kernels for 0% -> 0%
where the time goes in v1:
time: 909 us; the launch traced here: 907 us
  waiting for transfers between devices  429 us (47%)
  blocking collectives  223 us (25%)
  local copies, waits for them, and re-layouts  87.9 us (10%)
  other arithmetic  75.4 us (8%)
  matrix products  39.2 us (4%)
  loops' own time  36.2 us (4%)
  between operations  15.8 us (2%)
    ppermute x60, waiting for transfers between devices, gather_by_hops(): lax.ppermute(current, axis, [(i, (i + 1) % size) for i in range(size)])  342 us
    psum x3, blocking collectives, squares(): return lax.psum(jnp.sum(residual * residual, axis=(0, 2)), ('row', 'col'))  121 us
    reduce_scatter x4, waiting for transfers between devices, apply_operator(): lax.psum_scatter(gathered_sum, 'row', scatter_dimension=0, tiled=True)  86.9 us
    psum x2, blocking collectives, shards(): lax.psum(jnp.sum(direction * applied, axis=(0, 2)), ('row', 'col'))  78.8 us
    dot_general x48, matrix products, visit(): jnp.einsum('pab,psa->psb', weights, pieces[local_rows], precision=lax.Pre...  39.2 us
    another operation x4, loops' own time, apply_operator(): gathered_sum = lax.fori_loop(0, turns, visit, empty)  36.2 us
    convert_element_type x48, other arithmetic, group_weights(): inside = (indices < last).astype(jnp.float32)  32.7 us
    scatter-add x48, other arithmetic, visit(): return running.at[cols_group].add(product)  29.3 us
  transfers between devices with their start and end apart: 64, of which 63 were waited for; matrix products, arithmetic and copies ran while one was open for 1% of the time, Pallas kernels for 0%

profile of v1, /device:TPU:0, one launch (start us, length us, event | category | flops | bytes accessed | tf_op | source)
XLA Modules:
  0.0 907.1 jit_solution(4417572746136524923)
XLA Ops:
  7.8 6.6 collective-permute-done
  26.1 5.9 collective-permute-done.3
  32.0 5.9 collective-permute-done.4
  37.8 5.9 collective-permute-done.5
  43.7 5.9 collective-permute-done.6
  49.5 5.9 collective-permute-done.7
  55.4 5.9 collective-permute-done.8
  61.3 5.9 collective-permute-done.9
  90.6 18.3 %all_gather.6 = f32[32,3,256]{2,1,0:T(4,128)S(1)} all-gather(f32[2,3,256]{2,1,0:T(4,128)S(1)} %copy.11), channel_id=1, replica_groups=mesh['row'=2,'col'=16] {'col'}, dimensions={0}, use_global_device_ids=true | all-gather | bytes 104448 | tf_op jit(solution)/shard_map/all_gather | solution.py:37
  116.4 56.3 %while.40 = (s32[]{:T(128)}, f32[4,8,256]{2,1,0:T(8,128)S(1)}, s32[]{:T(128)}, s32[]{:T(128)}, s32[65]{0:T(128)S(1)}, /*index=5*/s32[65]{0:T(128)S(1)}, f32[32,8...) while((s32[]{:T(128)}, f32[4,8,256]{2,1,0:T(8,128)S(1)}, ...), condition=%wide.region_5.7_spmd, body=%wide.region_3.6_spmd.sunk | while | flops 14687269 | bytes 213307 | solution.py:79
  173.4 22.5 %reduce-scatter.5.cloned.1.call-done = f32[2,8,256]{2,1,0:T(8,128)} async-done(((f32[4,8,256]{2,1,0:T(8,128)}), f32[2,8,256]{2,1,0:T(8,128)}) %reduce-scatter.5.cloned.1.call-update) | async-done | bytes 16400 | tf_op jit(solution)/shard_map/reduce_scatter | solution.py:80
  284.8 56.3 %while.41 = (s32[]{:T(128)}, f32[4,8,256]{2,1,0:T(8,128)S(1)}, s32[]{:T(128)}, s32[]{:T(128)}, s32[65]{0:T(128)S(1)}, /*index=5*/s32[65]{0:T(128)S(1)}, f32[32,8...) while((s32[]{:T(128)}, f32[4,8,256]{2,1,0:T(8,128)S(1)}, ...), condition=%wide.region_11.13_spmd, body=%wide.region_9.12_spmd.sunk | while | flops 14687269 | bytes 213307 | solution.py:79
  341.8 20.1 %reduce-scatter.7.cloned.1.call-done = f32[2,8,256]{2,1,0:T(8,128)} async-done(((f32[4,8,256]{2,1,0:T(8,128)}), f32[2,8,256]{2,1,0:T(8,128)}) %reduce-scatter.7.cloned.1.call-update) | async-done | bytes 16400 | tf_op jit(solution)/shard_map/reduce_scatter | solution.py:80
  362.8 39.3 %all-reduce.2 = (f32[8]{0:T(128)S(1)}, f32[8]{0:T(128)S(1)}) all-reduce(f32[8]{0:T(128)S(1)} %get-tuple-element.222, f32[8]{0:T(128)S(1)} %get-tuple-element.221), channel_id=1, replica_groups=mesh['row'=2,'col'=16] {'row','col'}, use_global_device_ids=true, to_apply=%region_8.10 | all-reduce | flops 16 | bytes 128 | tf_op jit(solution)/shard_map/psum | solution.py:33
  402.3 41.0 %psum.44 = f32[8]{0:T(128)S(1)} all-reduce(f32[8]{0:T(128)S(1)} %multiply_reduce_fusion.3), channel_id=1, replica_groups=mesh['row'=2,'col'=16] {'row','col'}, use_global_device_ids=true, to_apply=%region_16.18 | all-reduce | flops 8 | bytes 64 | tf_op jit(solution)/shard_map/psum | solution.py:33
  443.4 5.9 collective-permute-done.30
  531.6 56.3 %while.42 = (s32[]{:T(128)}, f32[4,8,256]{2,1,0:T(8,128)S(1)}, s32[]{:T(128)}, s32[]{:T(128)}, s32[65]{0:T(128)S(1)}, /*index=5*/s32[65]{0:T(128)S(1)}, f32[32,8...) while((s32[]{:T(128)}, f32[4,8,256]{2,1,0:T(8,128)S(1)}, ...), condition=%wide.region_19.21_spmd, body=%wide.region_17.20_spmd.sunk | while | flops 14687269 | bytes 213307 | solution.py:79
  588.5 22.2 %reduce-scatter.9.cloned.1.call-done = f32[2,8,256]{2,1,0:T(8,128)} async-done(((f32[4,8,256]{2,1,0:T(8,128)}), f32[2,8,256]{2,1,0:T(8,128)}) %reduce-scatter.9.cloned.1.call-update) | async-done | bytes 16400 | tf_op jit(solution)/shard_map/reduce_scatter | solution.py:80
  611.6 39.5 %psum.45 = f32[8]{0:T(128)S(1)} all-reduce(f32[8]{0:T(128)S(1)} %multiply_reduce_fusion.2), channel_id=1, replica_groups=mesh['row'=2,'col'=16] {'row','col'}, use_global_device_ids=true, to_apply=%region_22.24 | all-reduce | flops 8 | bytes 64 | tf_op jit(solution)/shard_map/psum | solution.py:89
  651.3 40.9 %psum.46 = f32[8]{0:T(128)S(1)} all-reduce(f32[8]{0:T(128)S(1)} %get-tuple-element.307), channel_id=1, replica_groups=mesh['row'=2,'col'=16] {'row','col'}, use_global_device_ids=true, to_apply=%region_24.26 | all-reduce | flops 8 | bytes 64 | tf_op jit(solution)/shard_map/psum | solution.py:33
  692.3 5.9 collective-permute-done.45
  780.5 56.3 %while.43 = (s32[]{:T(128)}, f32[4,8,256]{2,1,0:T(8,128)S(1)}, s32[]{:T(128)}, s32[]{:T(128)}, s32[65]{0:T(128)S(1)}, /*index=5*/s32[65]{0:T(128)S(1)}, f32[32,8...) while((s32[]{:T(128)}, f32[4,8,256]{2,1,0:T(8,128)S(1)}, ...), condition=%wide.region_27.29_spmd, body=%wide.region_25.28_spmd.sunk | while | flops 14687269 | bytes 213307 | solution.py:79
  837.5 22.2 %reduce-scatter.11.cloned.1.call-done = f32[2,8,256]{2,1,0:T(8,128)} async-done(((f32[4,8,256]{2,1,0:T(8,128)}), f32[2,8,256]{2,1,0:T(8,128)}) %reduce-scatter.11.cloned.1.call-update) | async-done | bytes 16400 | tf_op jit(solution)/shard_map/reduce_scatter | solution.py:80
  860.6 39.3 %psum.47 = f32[8]{0:T(128)S(1)} all-reduce(f32[8]{0:T(128)S(1)} %multiply_reduce_fusion), channel_id=1, replica_groups=mesh['row'=2,'col'=16] {'row','col'}, use_global_device_ids=true, to_apply=%region_30.32 | all-reduce | flops 8 | bytes 64 | tf_op jit(solution)/shard_map/psum | solution.py:89
  (1101 shorter events, 490.4 us)
Async XLA Ops:
  7.2 188.7 %reduce-scatter.5.cloned.1.call-start = ((), (), s32[]{:S(2)}) async-start(), calls=%async_computation.4 | async-start | bytes 49152 | tf_op jit(solution)/shard_map/reduce_scatter | solution.py:80
  7.2 7.2 collective-permute-start
  37.8 5.9 collective-permute-start.5
  43.7 5.9 collective-permute-start.6
  49.5 5.9 collective-permute-start.7
  55.4 5.9 collective-permute-start.8
  61.3 5.9 collective-permute-start.9
  67.1 5.9 collective-permute-start.10
  73.0 5.9 collective-permute-start.11
  78.8 5.9 collective-permute-start.12
  84.7 5.9 collective-permute-start.13
  90.6 24.9 %collective-permute-start.14 = (f32[2,8,256]{2,1,0:T(8,128)S(1)}, f32[2,8,256]{2,1,0:T(8,128)S(1)}, u32[]{:S(2)}, u32[]{:S(2)}) collective-permute-start(f32[2,8,256]{2,1,0:T(8,128)S(1)} %collective-permute-done.13), channel_id=1, source_target_pairs={{0,1},{1,2},{2,3},{3,4},{4,5},{5,6},{6,7},{7,8},{8,9},{9,10},{10,1... | collective-permute-start | bytes 49160 | tf_op jit(solution)/shard_map/ppermute | solution.py:14
  173.3 188.5 %reduce-scatter.7.cloned.1.call-start = ((), (), s32[]{:S(2)}) async-start(), calls=%async_computation.5 | async-start | bytes 49152 | tf_op jit(solution)/shard_map/reduce_scatter | solution.py:80
  196.6 5.9 collective-permute-start.15
  202.5 5.9 collective-permute-start.16
  208.3 5.9 collective-permute-start.17
  214.2 5.9 collective-permute-start.18
  220.0 5.9 collective-permute-start.19
  225.9 5.9 collective-permute-start.20
  231.8 5.9 collective-permute-start.21
  341.7 269.0 %reduce-scatter.9.cloned.1.call-start = ((), (), s32[]{:S(2)}) async-start(), calls=%async_computation.6 | async-start | bytes 49152 | tf_op jit(solution)/shard_map/reduce_scatter | solution.py:80
  443.4 5.9 collective-permute-start.30
  588.5 271.2 %reduce-scatter.11.cloned.1.call-start = ((), (), s32[]{:S(2)}) async-start(), calls=%async_computation.7 | async-start | bytes 49152 | tf_op jit(solution)/shard_map/reduce_scatter | solution.py:80
  692.3 5.9 collective-permute-start.45
  (51 other events, 411.5 us)
Sparse Core Ops, SparseCore 0:
  173.4 22.3 reduce-scatter.4
  341.8 19.9 reduce-scatter.6
  588.6 22.0 reduce-scatter.8
  837.6 22.0 reduce-scatter.10
